TPU v7x, 128 devices: a whole 4x4x4 slice. The times are simulated.
128 devices in a mesh: gx: 8 (over y_lo, x), gy: 16 (over y_hi, z, core).
Axes of the slice: x: 4, y: 4 (y_hi: 2, y_lo: 2; y = y_hi * 2 + y_lo), z: 4, core: 2. Of those that a mesh axis runs over, the one named last changes fastest.
Arguments:
- patches: bfloat16 [1024, 6144], P('gy', 'gx'), may hold values from -2000 to 2000
- norm_gain: float32 [6144], P('gx'), may hold values from 0.5 to 1.5
- w_up: bfloat16 [6144, 24576], P('gx', 'gy'), may hold values from -0.078125 to 0.078125
- bias_up: float32 [24576], P('gy'), may hold values from -4 to 4
- w_down: bfloat16 [24576, 6144], P('gy', 'gx'), may hold values from -0.0390625 to 0.0390625
- bias_down: float32 [6144], P('gx'), may hold values from -4 to 4
- cotangent: bfloat16 [1024, 6144], P('gy', 'gx'), may hold values from -4 to 4
Outputs:
- mlp_out: bfloat16 [1024, 6144], P('gy', 'gx')
- grad_patches: bfloat16 [1024, 6144], P('gy', 'gx')
- grad_gain: float32 [6144], P('gx')
- grad_w_up: float32 [6144, 24576], P('gx', 'gy')
- grad_bias_up: float32 [24576], P('gy')
- grad_w_down: float32 [24576, 6144], P('gy', 'gx')
- grad_bias_down: float32 [6144], P('gx')
All inputs are finite; a program needn't handle non-finite values.
Results may differ from a plain program's by a relative error of at most 0.007.
Values may be sent and summed in bfloat16 or wider, within the bound.
A program may use at most 128 MiB of HBM per device.

v0:
```python
import jax
import jax.numpy as jnp
from jax import lax
from jax.sharding import PartitionSpec as P

D = 6144
epsilon = 1e-06
inv_root_two = 0.7071067811865476
inv_root_two_pi = 0.3989422804014327


def gelu_value(hidden):
    return 0.5 * hidden * (1.0 + lax.erf(hidden * inv_root_two))


def gelu_slope(hidden):
    return (
        0.5 * (1.0 + lax.erf(hidden * inv_root_two))
        + hidden * jnp.exp(-0.5 * hidden * hidden) * inv_root_two_pi
    )


def over_rows(left, right):
    return lax.dot_general(
        left, right, (((0,), (0,)), ((), ())), preferred_element_type=jnp.float32
    )


def over_cols(left, right):
    return lax.dot_general(
        left, right, (((1,), (1,)), ((), ())), preferred_element_type=jnp.float32
    )


def shards(patches, norm_gain, w_up, bias_up, w_down, bias_down, cotangent):
    values = patches.astype(jnp.float32)
    row_total, row_squares = lax.psum(
        (jnp.sum(values, axis=1), jnp.sum(values * values, axis=1)), "gx"
    )
    row_mean = (row_total / D)[:, None]
    variance = (row_squares / D)[:, None] - row_mean * row_mean
    inv_std = lax.rsqrt(variance + epsilon)
    standard = (values - row_mean) * inv_std
    normed = (standard * norm_gain).astype(jnp.bfloat16)
    partial_value = jnp.dot(
        lax.all_gather(normed, "gy", axis=0, tiled=True), w_up, preferred_element_type=jnp.float32
    )
    hidden = lax.psum(partial_value, "gx") + bias_up
    act_whole = gelu_value(hidden).astype(jnp.bfloat16)
    block = act_whole
    mlp_out = (
        lax.psum_scatter(
            jnp.dot(block, w_down, preferred_element_type=jnp.float32),
            "gy",
            scatter_dimension=0,
            tiled=True,
        )
        + bias_down
    ).astype(jnp.bfloat16)
    piece = lax.all_gather(cotangent, "gy", axis=0, tiled=True)
    weight_total = over_rows(act_whole, piece)
    act_grads = over_cols(piece, w_down)
    grad_act = lax.psum(act_grads, "gx")
    grad_whole = (grad_act * gelu_slope(hidden)).astype(jnp.bfloat16)
    grad_bias_up = jnp.sum(grad_whole, axis=0, dtype=jnp.float32)
    grad_w_up = over_rows(lax.all_gather(normed, "gy", axis=0, tiled=True), grad_whole)
    block = grad_whole
    grad_normed = lax.psum_scatter(over_cols(block, w_up), "gy", scatter_dimension=0, tiled=True)
    grad_gain, grad_bias_down = lax.psum(
        (jnp.sum(grad_normed * standard, axis=0), jnp.sum(cotangent, axis=0, dtype=jnp.float32)),
        "gy",
    )
    scaled = grad_normed * norm_gain
    first_total, second_total = lax.psum(
        (jnp.sum(scaled, axis=1), jnp.sum(scaled * standard, axis=1)), "gx"
    )
    first_mean = (first_total / D)[:, None]
    second_mean = (second_total / D)[:, None]
    grad_patches = (inv_std * (scaled - first_mean - standard * second_mean)).astype(jnp.bfloat16)
    return (mlp_out, grad_patches, grad_gain, grad_w_up, grad_bias_up, weight_total, grad_bias_down)


def solution(mesh):
    in_specs = (
        P("gy", "gx"),
        P("gx"),
        P("gx", "gy"),
        P("gy"),
        P("gy", "gx"),
        P("gx"),
        P("gy", "gx"),
    )
    out_specs = (
        P("gy", "gx"),
        P("gy", "gx"),
        P("gx"),
        P("gx", "gy"),
        P("gy"),
        P("gy", "gx"),
        P("gx"),
    )
    return jax.shard_map(shards, mesh=mesh, in_specs=in_specs, out_specs=out_specs, check_vma=False)
```

profile of v0, /device:TPU:0, one launch (start us, length us, event | category | flops | bytes accessed | tf_op | source)
XLA Modules:
  0.0 570.0 jit_solution(7899502057630705862)
XLA Ops:
  7.2 0.0 all-gather.3.cloned.1.call-start
  7.2 1.2 convert_reduce_fusion.1
  8.4 19.8 %all-reduce.2 = (f32[64]{0:T(128)S(1)}, f32[64]{0:T(128)S(1)}) all-reduce(f32[64]{0:T(128)S(1)} %get-tuple-element.11, f32[64]{0:T(128)S(1)} %get-tuple-element.10), channel_id=1, replica_groups=mesh['gx'=8,'gy'=16] {'gx'}, use_global_device_ids=true, to_apply=%region_3.0 | all-reduce | flops 128 | bytes 1024 | tf_op jit(solution)/shard_map/psum | solution.py:37
  28.2 1.6 fusion.11
  29.9 0.0 all-gather.3.cloned.1.call-update
  29.9 0.0 all-gather.5.cloned.1.call-start
  29.9 0.7 all-gather.5.cloned.1.call-update
  30.6 0.0 all-reduce.6.cloned.1.call-start
  30.7 45.4 %all-gather.3.cloned.1.call-done = bf16[1024,768]{1,0:T(8,128)(2,1)} async-done(((bf16[64,768]{1,0:T(8,128)(2,1)}), bf16[1024,768]{1,0:T(8,128)(2,1)}) %all-gather.3.cloned.1.call-update) | async-done | bytes 1572880 | tf_op jit(solution)/shard_map/all_gather | solution.py:46
  76.0 5.9 %fusion.19 = f32[1024,1536]{1,0:T(8,128)} fusion(bf16[1024,768]{1,0:T(8,128)(2,1)} %all-gather.3.cloned.1.call-done, bf16[768,1536]{1,0:T(8,128)(2,1)S(1)} %copy-done), kind=kOutput, calls=%fused_computation.32 | convolution fusion | flops 2415919104 | bytes 10223616 | tf_op jit(solution)/shard_map/dot_general | solution.py:45
  81.9 41.7 %all-gather.5.cloned.1.call-done = bf16[1024,768]{1,0:T(8,128)(2,1)} async-done(((bf16[64,768]{1,0:T(8,128)(2,1)}), bf16[1024,768]{1,0:T(8,128)(2,1)}) %all-gather.5.cloned.1.call-update) | async-done | bytes 1572880 | tf_op jit(solution)/shard_map/all_gather | solution.py:60
  123.6 7.4 %fusion.21 = f32[1024,1536]{1,0:T(8,128)} fusion(bf16[1024,768]{1,0:T(8,128)(2,1)} %all-gather.5.cloned.1.call-done, bf16[1536,768]{1,0:T(8,128)(2,1)} %param.11), kind=kOutput, calls=%fused_computation.34 | convolution fusion | flops 2415919104 | bytes 10223616 | tf_op jit(solution)/shard_map/dot_general | solution.py:30
  131.0 0.0 all-reduce.6.cloned.1.call-update
  131.0 0.0 reduce-scatter.5.cloned.1.call-start
  131.1 262.5 %all-reduce.6.cloned.1.call-done = (f32[1024,1536]{1,0:T(8,128)}, f32[1024,1536]{1,0:T(8,128)}) async-done(((f32[1024,1536]{1,0:T(8,128)}, f32[1024,1536]{1,0:T(8,128)}), (f32[1024,1536]{1,0:T(8,128)}, f32[1024,1536]{1,0:T(8,128)})) %all-reduce.6.cloned.1.call-update) | async-done | bytes 12582928 | tf_op jit(solution)/shard_map/psum | solution.py:48
  393.6 9.2 %convert_reduce_fusion = (f32[1536]{0:T(1024)}, bf16[1024,1536]{1,0:T(8,128)(2,1)S(1)}, bf16[1024,1536]{1,0:T(8,128)(2,1)}) fusion(f32[1024,1536]{1,0:T(8,128)} %get-tuple-element.19, f32[1024,1536]{1,0:T(8,128)} %get-tuple-element.18, f32[1536]{0:T(1024)S(1)} %copy-done.6), kind=kLoop, calls=%fused_computation.7 | loop fusion | flops 25164288 | bytes 18886656 | tf_op jit(solution)/shard_map/reduce_sum | solution.py:65
  402.8 1.7 copy-done.1
  404.5 4.3 fusion.22
  408.8 0.0 reduce-scatter.5.cloned.1.call-update
  408.8 0.0 reduce-scatter.3.cloned.1.call-start
  408.9 6.9 %fusion.20 = f32[1024,768]{1,0:T(8,128)} fusion(bf16[1024,1536]{1,0:T(8,128)(2,1)} %get-tuple-element.22, bf16[1536,768]{1,0:T(8,128)(2,1)} %param.11), kind=kOutput, calls=%fused_computation.33 | convolution fusion | flops 2415919104 | bytes 8650752 | tf_op jit(solution)/shard_map/dot_general | solution.py:53
  415.8 0.0 reduce-scatter.3.cloned.1.call-update
  415.8 0.9 copy-done.4
  416.7 7.5 %fusion.23 = f32[768,1536]{1,0:T(8,128)} fusion(bf16[1024,768]{1,0:T(8,128)(2,1)} %all-gather.3.cloned.1.call-done, bf16[1024,1536]{1,0:T(8,128)(2,1)} %copy-done.1), kind=kOutput, calls=%fused_computation.36 | convolution fusion | flops 2415919104 | bytes 9437184 | tf_op jit(solution)/shard_map/dot_general | solution.py:24
  424.3 4.4 fusion.24
  428.6 54.9 %reduce-scatter.5.cloned.1.call-done = f32[64,768]{1,0:T(8,128)} async-done(((f32[1024,768]{1,0:T(8,128)}), f32[64,768]{1,0:T(8,128)}) %reduce-scatter.5.cloned.1.call-update) | async-done | bytes 196624 | tf_op jit(solution)/shard_map/reduce_scatter | solution.py:68
  483.5 1.2 fusion.16
  484.7 18.7 %all-reduce.1 = (f32[64]{0:T(128)S(1)}, f32[64]{0:T(128)S(1)}) all-reduce(f32[64]{0:T(128)S(1)} %get-tuple-element.8, f32[64]{0:T(128)S(1)} %get-tuple-element.9), channel_id=1, replica_groups=mesh['gx'=8,'gy'=16] {'gx'}, use_global_device_ids=true, to_apply=%region_11.0 | all-reduce | flops 128 | bytes 1024 | tf_op jit(solution)/shard_map/psum | solution.py:74
  503.3 34.6 %all-reduce = (f32[768]{0:T(1024)}, f32[768]{0:T(1024)}) all-reduce(f32[768]{0:T(1024)S(1)} %get-tuple-element.7, f32[768]{0:T(1024)S(1)} %convert_reduce_fusion.2), channel_id=1, replica_groups=mesh['gx'=8,'gy'=16] {'gy'}, use_global_device_ids=true, to_apply=%region_13.0 | all-reduce | flops 1536 | bytes 12288 | tf_op jit(solution)/shard_map/psum | solution.py:69
  538.0 1.7 fusion.15
  539.7 22.2 %reduce-scatter.3.cloned.1.call-done = f32[64,768]{1,0:T(8,128)} async-done(((f32[1024,768]{1,0:T(8,128)}), f32[64,768]{1,0:T(8,128)}) %reduce-scatter.3.cloned.1.call-update) | async-done | bytes 196624 | tf_op jit(solution)/shard_map/reduce_scatter | solution.py:52
  561.9 1.6 add_convert_fusion
  (19 shorter events, 0.1 us)
Async XLA Ops:
  7.2 68.9 %copy-start = (bf16[768,1536]{1,0:T(8,128)(2,1)S(1)}, bf16[768,1536]{1,0:T(8,128)(2,1)}, u32[]{:S(2)}) copy-start(bf16[768,1536]{1,0:T(8,128)(2,1)} %param.9) | copy-start | bytes 7077892
  7.2 68.9 %all-gather.3.cloned.1.call-start = ((), (), s32[]{:S(2)}) async-start(), calls=%async_computation.2 | async-start | bytes 1671168 | tf_op jit(solution)/shard_map/all_gather | solution.py:46
  29.9 93.8 %all-gather.5.cloned.1.call-start = ((), (), s32[]{:S(2)}) async-start(), calls=%async_computation.4 | async-start | bytes 1671168 | tf_op jit(solution)/shard_map/all_gather | solution.py:60
  30.6 363.0 %all-reduce.6.cloned.1.call-start = ((), (), s32[]{:S(2)}) async-start(), calls=%async_computation.6 | async-start | bytes 25165824 | tf_op jit(solution)/shard_map/psum | solution.py:48
  131.0 262.6 %copy-start.6 = (f32[1536]{0:T(1024)S(1)}, f32[1536]{0:T(1024)}, u32[]{:S(2)}) copy-start(f32[1536]{0:T(1024)} %param.10) | copy-start | bytes 18436
  131.0 352.5 %reduce-scatter.5.cloned.1.call-start = ((), (), s32[]{:S(2)}) async-start(), calls=%async_computation.5 | async-start | bytes 3342336 | tf_op jit(solution)/shard_map/reduce_scatter | solution.py:68
  402.8 1.7 copy-start.1
  408.8 153.1 %reduce-scatter.3.cloned.1.call-start = ((), (), s32[]{:S(2)}) async-start(), calls=%async_computation.3 | async-start | bytes 3342336 | tf_op jit(solution)/shard_map/reduce_scatter | solution.py:52
  415.8 0.9 copy-start.4
  416.7 7.5 %copy-start.2 = (bf16[1024,1536]{1,0:T(8,128)(2,1)S(1)}, bf16[1024,1536]{1,0:T(8,128)(2,1)}, u32[]{:S(2)}) copy-start(bf16[1024,1536]{1,0:T(8,128)(2,1)} %get-tuple-element.22) | copy-start | bytes 9437188
  416.7 7.5 %copy-start.8 = (bf16[1024,768]{1,0:T(8,128)(2,1)S(1)}, bf16[1024,768]{1,0:T(8,128)(2,1)}, u32[]{:S(2)}) copy-start(bf16[1024,768]{1,0:T(8,128)(2,1)} %all-gather.5.cloned.1.call-done) | copy-start | bytes 4718596
  424.2 59.3 %copy-start.3 = (bf16[64,768]{1,0:T(8,128)(2,1)S(1)}, bf16[64,768]{1,0:T(8,128)(2,1)}, u32[]{:S(2)}) copy-start(bf16[64,768]{1,0:T(8,128)(2,1)} %param.7) | copy-start | bytes 294916
  424.2 59.3 %copy-start.5 = (f32[768]{0:T(1024)S(1)}, f32[768]{0:T(1024)}, u32[]{:S(2)}) copy-start(f32[768]{0:T(1024)} %param.8) | copy-start | bytes 9220
  424.2 137.7 %copy-start.7 = (f32[768]{0:T(1024)S(1)}, f32[768]{0:T(1024)}, u32[]{:S(2)}) copy-start(f32[768]{0:T(1024)} %param.12) | copy-start | bytes 9220
Sparse Core Ops, SparseCore 0:
  30.0 45.9 all-gather.2
  78.5 45.0 all-gather.4
  131.2 262.3 all-reduce.5
  408.9 74.5 reduce-scatter.4
  487.4 74.4 reduce-scatter.2
where the time goes:
time: 570 us
  waiting for transfers between devices  427 us (75%)
  blocking collectives  73.1 us (13%)
  matrix products  36.4 us (6%)
  other arithmetic  16.4 us (3%)
  between operations  13.8 us (2%)
    psum x1, waiting for transfers between devices, shards(): hidden = lax.psum(partial_value, 'gx') + bias_up  263 us
    reduce_scatter x1, waiting for transfers between devices, shards(): lax.psum_scatter(over_cols(block, w_up), 'gy', scatter_dimension=0, tiled...  54.9 us
    all_gather x1, waiting for transfers between devices, shards(): lax.all_gather(normed, 'gy', axis=0, tiled=True)  45.4 us
    all_gather x1, waiting for transfers between devices, shards(): piece = lax.all_gather(cotangent, 'gy', axis=0, tiled=True)  41.7 us
    psum x1, blocking collectives, shards(): lax.psum((jnp.sum(grad_normed * standard, axis=0), jnp.sum(cotangent, axi...  34.6 us
    reduce_scatter x1, waiting for transfers between devices, shards(): lax.psum_scatter(jnp.dot(block, w_down, preferred_element_type=jnp.float3...  22.2 us
    psum x1, blocking collectives, shards(): lax.psum((jnp.sum(values, axis=1), jnp.sum(values * values, axis=1)), 'gx')  19.8 us
    psum x1, blocking collectives, shards(): lax.psum((jnp.sum(scaled, axis=1), jnp.sum(scaled * standard, axis=1)), '...  18.7 us
  transfers between devices with their start and end apart: 5, of which 5 were waited for; matrix products, arithmetic and copies ran while one was open for 5% of the time, Pallas kernels for 0%

commit v1 on v0

--- a/solution.py
+++ b/solution.py
@@ -7,6 +7,7 @@
 epsilon = 1e-06
 inv_root_two = 0.7071067811865476
 inv_root_two_pi = 0.3989422804014327
+meet_pipes_all = lambda inputs: jnp.sum(lax.all_gather(inputs, axis_name="gx"), axis=0)
 
 
 def gelu_value(hidden):
@@ -45,7 +46,7 @@
     partial_value = jnp.dot(
         lax.all_gather(normed, "gy", axis=0, tiled=True), w_up, preferred_element_type=jnp.float32
     )
-    hidden = lax.psum(partial_value, "gx") + bias_up
+    hidden = meet_pipes_all(partial_value) + bias_up
     act_whole = gelu_value(hidden).astype(jnp.bfloat16)
     block = act_whole
     mlp_out = (

time: 570 us -> 932 us (1.64)
  waiting for transfers between devices: 427 us -> 766 us
  other arithmetic: 16.4 us -> 38.7 us
    all_gather x0 -> x1, waiting for transfers between devices: none -> 478 us  [lax.all_gather(inputs, axis_name='gx')]
    psum x1, waiting for transfers between devices: 263 us -> 124 us  [shards(): grad_act = lax.psum(act_grads, 'gx')]
    reduce_sum x0 -> x1, other arithmetic: none -> 22.3 us  [jnp.sum(lax.all_gather(inputs, axis_name='gx'), axis=0)]
  transfers between devices with their start and end apart: 5 -> 6, of which waited for: 5 -> 6; matrix products, arithmetic and copies ran while one was open for 5% -> 6% of each run, Pallas kernels for 0% -> 0%
where the time goes in v1:
time: 932 us
  waiting for transfers between devices  766 us (82%)
  blocking collectives  73.2 us (8%)
  other arithmetic  38.7 us (4%)
  matrix products  36.4 us (4%)
  between operations  14.2 us (2%)
    all_gather x1, waiting for transfers between devices, lax.all_gather(inputs, axis_name='gx')  478 us
    psum x1, waiting for transfers between devices, shards(): grad_act = lax.psum(act_grads, 'gx')  124 us
    reduce_scatter x1, waiting for transfers between devices, shards(): lax.psum_scatter(over_cols(block, w_up), 'gy', scatter_dimension=0, tiled...  54.6 us
    all_gather x1, waiting for transfers between devices, shards(): lax.all_gather(normed, 'gy', axis=0, tiled=True)  45.4 us
    all_gather x1, waiting for transfers between devices, shards(): piece = lax.all_gather(cotangent, 'gy', axis=0, tiled=True)  41.7 us
    psum x1, blocking collectives, shards(): lax.psum((jnp.sum(grad_normed * standard, axis=0), jnp.sum(cotangent, axi...  34.7 us
    reduce_sum x1, other arithmetic, jnp.sum(lax.all_gather(inputs, axis_name='gx'), axis=0)  22.3 us
    reduce_scatter x1, waiting for transfers between devices, shards(): lax.psum_scatter(jnp.dot(block, w_down, preferred_element_type=jnp.float3...  22.2 us
  transfers between devices with their start and end apart: 6, of which 6 were waited for; matrix products, arithmetic and copies ran while one was open for 6% of the time, Pallas kernels for 0%

profile of v1, /device:TPU:0, one launch (start us, length us, event | category | flops | bytes accessed | tf_op | source)
XLA Modules:
  0.0 931.7 jit_solution(6520909556004952064)
XLA Ops:
  7.2 0.0 all-gather.5.cloned.1.call-start
  7.2 1.2 convert_reduce_fusion.1
  8.4 19.8 %all-reduce.2 = (f32[64]{0:T(128)S(1)}, f32[64]{0:T(128)S(1)}) all-reduce(f32[64]{0:T(128)S(1)} %get-tuple-element.11, f32[64]{0:T(128)S(1)} %get-tuple-element.10), channel_id=1, replica_groups=mesh['gx'=8,'gy'=16] {'gx'}, use_global_device_ids=true, to_apply=%region_3.0 | all-reduce | flops 128 | bytes 1024 | tf_op jit(solution)/shard_map/psum | solution.py:38
  28.2 1.6 fusion.11
  29.9 0.0 all-gather.5.cloned.1.call-update
  29.9 0.0 all-gather.7.cloned.1.call-start
  29.9 0.7 all-gather.7.cloned.1.call-update
  30.6 0.0 all-gather.9.cloned.1.call-start
  30.7 45.4 %all-gather.5.cloned.1.call-done = bf16[1024,768]{1,0:T(8,128)(2,1)} async-done(((bf16[64,768]{1,0:T(8,128)(2,1)}), bf16[1024,768]{1,0:T(8,128)(2,1)}) %all-gather.5.cloned.1.call-update) | async-done | bytes 1572880 | tf_op jit(solution)/shard_map/all_gather | solution.py:47
  76.0 5.9 fusion.19
  81.9 0.0 all-reduce.5.cloned.1.call-start
  82.0 41.7 %all-gather.7.cloned.1.call-done = bf16[1024,768]{1,0:T(8,128)(2,1)} async-done(((bf16[64,768]{1,0:T(8,128)(2,1)}), bf16[1024,768]{1,0:T(8,128)(2,1)}) %all-gather.7.cloned.1.call-update) | async-done | bytes 1572880 | tf_op jit(solution)/shard_map/all_gather | solution.py:61
  123.6 7.4 fusion.21
  131.0 0.0 reduce-scatter.5.cloned.1.call-start
  131.1 478.0 %all-gather.9.cloned.1.call-done = f32[8192,1536]{1,0:T(8,128)} async-done(((f32[1024,1536]{1,0:T(8,128)}), f32[8192,1536]{1,0:T(8,128)}) %all-gather.9.cloned.1.call-update) | async-done | bytes 50331664 | tf_op jit(solution)/shard_map/all_gather | solution.py:10
  609.1 22.3 %reduce_sum.74 = f32[1024,1536]{1,0:T(8,128)} reduce(f32[8,1024,1536]{2,1,0:T(8,128)} %bitcast.13, f32[]{:T(128)} %constant.4.clone.1), dimensions={0}, to_apply=%region_4.0 | reduce | flops 11010048 | bytes 56623108 | tf_op jit(solution)/shard_map/reduce_sum | solution.py:10
  631.4 123.7 %all-reduce.5.cloned.1.call-done = f32[1024,1536]{1,0:T(8,128)} async-done(((f32[1024,1536]{1,0:T(8,128)}), f32[1024,1536]{1,0:T(8,128)}) %all-reduce.5.cloned.1.call-update) | async-done | bytes 6291472 | tf_op jit(solution)/shard_map/psum | solution.py:64
  755.1 9.2 convert_reduce_fusion
  764.3 1.7 copy-done.1
  766.0 4.3 fusion.22
  770.4 0.2 reduce-scatter.3.cloned.1.call-start
  770.6 6.9 fusion.20
  777.5 0.9 copy-done.4
  778.4 7.5 fusion.23
  786.0 4.4 fusion.24
  790.4 54.6 %reduce-scatter.5.cloned.1.call-done = f32[64,768]{1,0:T(8,128)} async-done(((f32[1024,768]{1,0:T(8,128)}), f32[64,768]{1,0:T(8,128)}) %reduce-scatter.5.cloned.1.call-update) | async-done | bytes 196624 | tf_op jit(solution)/shard_map/reduce_scatter | solution.py:69
  844.9 1.2 fusion.16
  846.1 18.7 %all-reduce.1 = (f32[64]{0:T(128)S(1)}, f32[64]{0:T(128)S(1)}) all-reduce(f32[64]{0:T(128)S(1)} %get-tuple-element.8, f32[64]{0:T(128)S(1)} %get-tuple-element.9), channel_id=1, replica_groups=mesh['gx'=8,'gy'=16] {'gx'}, use_global_device_ids=true, to_apply=%region_11.0 | all-reduce | flops 128 | bytes 1024 | tf_op jit(solution)/shard_map/psum | solution.py:75
  864.8 34.7 %all-reduce = (f32[768]{0:T(1024)}, f32[768]{0:T(1024)}) all-reduce(f32[768]{0:T(1024)S(1)} %get-tuple-element.7, f32[768]{0:T(1024)S(1)} %convert_reduce_fusion.2), channel_id=1, replica_groups=mesh['gx'=8,'gy'=16] {'gy'}, use_global_device_ids=true, to_apply=%region_13.0 | all-reduce | flops 1536 | bytes 12288 | tf_op jit(solution)/shard_map/psum | solution.py:70
  899.4 1.7 fusion.15
  901.1 22.2 %reduce-scatter.3.cloned.1.call-done = f32[64,768]{1,0:T(8,128)} async-done(((f32[1024,768]{1,0:T(8,128)}), f32[64,768]{1,0:T(8,128)}) %reduce-scatter.3.cloned.1.call-update) | async-done | bytes 196624 | tf_op jit(solution)/shard_map/reduce_scatter | solution.py:53
  923.3 1.6 add_convert_fusion
  (23 shorter events, 0.1 us)
Async XLA Ops:
  7.2 68.9 %copy-start = (bf16[768,1536]{1,0:T(8,128)(2,1)S(1)}, bf16[768,1536]{1,0:T(8,128)(2,1)}, u32[]{:S(2)}) copy-start(bf16[768,1536]{1,0:T(8,128)(2,1)} %param.9) | copy-start | bytes 7077892
  7.2 68.9 %all-gather.5.cloned.1.call-start = ((), (), s32[]{:S(2)}) async-start(), calls=%async_computation.2 | async-start | bytes 1671168 | tf_op jit(solution)/shard_map/all_gather | solution.py:47
  29.9 93.8 %all-gather.7.cloned.1.call-start = ((), (), s32[]{:S(2)}) async-start(), calls=%async_computation.4 | async-start | bytes 1671168 | tf_op jit(solution)/shard_map/all_gather | solution.py:61
  30.6 578.5 %all-gather.9.cloned.1.call-start = ((), (), s32[]{:S(2)}) async-start(), calls=%async_computation.7 | async-start | bytes 56623104 | tf_op jit(solution)/shard_map/all_gather | solution.py:10
  81.9 673.2 %all-reduce.5.cloned.1.call-start = ((), (), s32[]{:S(2)}) async-start(), calls=%async_computation.5 | async-start | bytes 12582912 | tf_op jit(solution)/shard_map/psum | solution.py:64
  131.0 713.9 %reduce-scatter.5.cloned.1.call-start = ((), (), s32[]{:S(2)}) async-start(), calls=%async_computation.6 | async-start | bytes 3342336 | tf_op jit(solution)/shard_map/reduce_scatter | solution.py:69
  609.1 146.0 %copy-start.6 = (f32[1536]{0:T(1024)S(1)}, f32[1536]{0:T(1024)}, u32[]{:S(2)}) copy-start(f32[1536]{0:T(1024)} %param.10) | copy-start | bytes 18436
  764.3 1.7 copy-start.1
  770.4 152.9 %reduce-scatter.3.cloned.1.call-start = ((), (), s32[]{:S(2)}) async-start(), calls=%async_computation.3 | async-start | bytes 3342336 | tf_op jit(solution)/shard_map/reduce_scatter | solution.py:53
  777.5 0.9 copy-start.4
  778.4 7.5 copy-start.2
  778.4 7.5 copy-start.8
  785.9 59.0 %copy-start.3 = (bf16[64,768]{1,0:T(8,128)(2,1)S(1)}, bf16[64,768]{1,0:T(8,128)(2,1)}, u32[]{:S(2)}) copy-start(bf16[64,768]{1,0:T(8,128)(2,1)} %param.7) | copy-start | bytes 294916
  786.0 59.0 %copy-start.5 = (f32[768]{0:T(1024)S(1)}, f32[768]{0:T(1024)}, u32[]{:S(2)}) copy-start(f32[768]{0:T(1024)} %param.8) | copy-start | bytes 9220
  786.0 137.3 %copy-start.7 = (f32[768]{0:T(1024)S(1)}, f32[768]{0:T(1024)}, u32[]{:S(2)}) copy-start(f32[768]{0:T(1024)} %param.12) | copy-start | bytes 9220
Sparse Core Ops, SparseCore 0:
  30.0 45.9 all-gather.4
  78.5 45.0 all-gather.6
  125.3 483.7 all-gather.8
  611.5 143.5 all-reduce.4
  770.5 74.3 reduce-scatter.4
  848.8 74.4 reduce-scatter.2
